TPU v7x, 32 devices: a whole 2x2x4 slice. The times are simulated.
32 devices in a mesh: dp: 8 (over z, y), tensor: 4 (over x, core).
Axes of the slice: x: 2, y: 2, z: 4, core: 2. Of those that a mesh axis runs over, the one named last changes fastest.
Arguments:
- tokens: bfloat16 [1024, 2048], P('dp'), may hold values from -6 to 6
- lengths: int32 [8], replicated, may hold values from 96 to 128, as said below
- request_adapter: int32 [8], replicated, may hold values from 0 to 63
- token_experts: int32 [1024, 8], P('dp'), may hold values from 0 to 63, as said below
- router_weight: float32 [1024, 8], P('dp'), may hold values from 0.05 to 1
- gate_weight: bfloat16 [128, 2048, 512], P('dp', None, 'tensor'), may hold values from -0.125 to 0.125
- up_weight: bfloat16 [128, 2048, 512], P('dp', None, 'tensor'), may hold values from -0.125 to 0.125
- down_weight: bfloat16 [128, 2048, 512], P('dp', None, 'tensor'), may hold values from -0.1875 to 0.1875
- adapter_input_maps: bfloat16 [2048, 2048], P('tensor', 'dp'), may hold values from -0.125 to 0.125
- adapter_output_maps: bfloat16 [2048, 2, 512], P('dp', None, 'tensor'), may hold values from -1.5 to 1.5
Outputs:
- moe_output: bfloat16 [1024, 2048], P('dp', 'tensor')
Inputs may be any that keep to these rules, and one draw needn't show every extreme that they name: `token_experts`: each row names 8 different experts. Among the rows of one request window, each expert is named by at most 28 rows, and one expert, the same in every window, is named by exactly 28 rows, all of live tokens. `lengths`: some request has all 128 tokens live.
All inputs are finite; a program needn't handle non-finite values.
Results may differ from a plain program's by a relative error of at most 0.0065.
Values may be sent and summed in bfloat16 or wider, within the bound.
No kernel may reach another device: no remote copies, remote signals or barrier semaphores. Data moves between devices by JAX's collectives and lax.ppermute only.
A program may use at most 320 MiB of HBM per device.

v0:
```python
import jax
import jax.numpy as jnp
from jax import lax
from jax.sharding import PartitionSpec as P

ADAPTER_RANK = 16
CAP = 28


def combine_routes(unit_table, lower_slot, shift_half, route_gain, tok_rows, topk):
    lower_slot = lower_slot.reshape(tok_rows, topk)
    route_gain = route_gain.reshape(tok_rows, topk)
    pair_slots = jnp.stack([lower_slot, lower_slot + shift_half], axis=2)
    pair_rows = unit_table[pair_slots].astype(jnp.float32)
    summed_pair = jnp.sum(pair_rows, axis=2)
    return jnp.sum(summed_pair * route_gain[:, :, None], axis=1)


def per_device(
    tokens,
    lengths,
    request_adapter,
    token_experts,
    router_weight,
    gate_weight,
    up_weight,
    down_weight,
    adapter_input_maps,
    adapter_output_maps,
):
    tok_rows, width = tokens.shape
    topk = token_experts.shape[1]
    dp_count = lax.axis_size("dp")
    tp_count = lax.axis_size("tensor")
    units_local = gate_weight.shape[0]
    experts_all = units_local * dp_count // 2
    quarter = CAP // tp_count
    double_rank = 2 * ADAPTER_RANK
    row_index = lax.axis_index("dp")
    part_index = lax.axis_index("tensor")
    live_mask = jnp.arange(tok_rows) < lengths[row_index]
    adapter = request_adapter[row_index]
    width_part = width // tp_count
    x_part = lax.dynamic_slice_in_dim(tokens, part_index * width_part, width_part, 1)
    device_portion = lax.all_gather(adapter_input_maps, "dp", axis=1, tiled=True)
    columns = jnp.arange(device_portion.shape[1])
    selector = (
        columns[:, None] == adapter * double_rank + jnp.arange(double_rank)[None, :]
    ).astype(jnp.bfloat16)
    chosen = jnp.dot(device_portion, selector, preferred_element_type=jnp.float32)
    partial_z = jnp.dot(x_part, chosen.astype(jnp.bfloat16), preferred_element_type=jnp.float32)
    low_rank = lax.psum(partial_z, "tensor").astype(jnp.bfloat16)
    entries = tok_rows * topk
    flat_ids = token_experts.reshape(entries)
    entry_token = jnp.arange(entries) // topk
    entry_live = live_mask[entry_token]
    expert_hits = (
        (flat_ids[:, None] == jnp.arange(experts_all)[None, :]) & entry_live[:, None]
    ).astype(jnp.int32)
    position = jnp.sum(jnp.cumsum(expert_hits, axis=0) * expert_hits, axis=1) - 1
    entry_mine = entry_live & (position // quarter == part_index)
    empty_slot = experts_all * quarter
    slot_part = jnp.where(entry_mine, flat_ids * quarter + position % quarter, empty_slot)
    slot_token = (
        jnp.full((empty_slot + 1,), tok_rows, jnp.int32).at[slot_part].set(entry_token)[:empty_slot]
    )
    padded_x = jnp.concatenate([tokens, jnp.zeros((1, width), jnp.bfloat16)], axis=0)
    padded_z = jnp.concatenate([low_rank, jnp.zeros((1, double_rank), jnp.bfloat16)], axis=0)
    slot_rows = padded_x[slot_token]
    slot_low = padded_z[slot_token]
    send_rows = jnp.concatenate([slot_rows, slot_rows], axis=0).reshape(
        dp_count, units_local, quarter, width
    )
    send_low = jnp.concatenate([slot_low, slot_low], axis=0).reshape(
        dp_count, units_local, quarter, double_rank
    )
    recv_rows, recv_low = (
        lax.all_to_all(send_rows, "dp", split_axis=0, concat_axis=0, tiled=True),
        lax.all_to_all(send_low, "dp", split_axis=0, concat_axis=0, tiled=True),
    )
    every_table = lax.all_gather(adapter_output_maps, "dp", axis=0, tiled=True)
    unit_half = (row_index * units_local + jnp.arange(units_local)) // experts_all
    half_tables = jnp.moveaxis(jnp.take(every_table, unit_half, axis=1), 1, 0)
    source_rows = (
        request_adapter[:, None] * double_rank + jnp.arange(double_rank)[None, :]
    ).reshape(dp_count * double_rank)
    source_tables = jnp.take(half_tables, source_rows, axis=1)
    gate_piece = lax.all_gather(gate_weight, "tensor", axis=2, tiled=True)
    up_piece = lax.all_gather(up_weight, "tensor", axis=2, tiled=True)
    table_piece = lax.all_gather(source_tables, "tensor", axis=2, tiled=True)
    table_split = table_piece.reshape(units_local, dp_count, double_rank, table_piece.shape[2])
    gate_term = jnp.einsum(
        "slcd,ldk->slck", recv_rows, gate_piece, preferred_element_type=jnp.float32
    )
    gate_term = gate_term + jnp.einsum(
        "slcj,lsjk->slck",
        recv_low[..., :ADAPTER_RANK],
        table_split[:, :, :ADAPTER_RANK],
        preferred_element_type=jnp.float32,
    )
    up_term = jnp.einsum("slcd,ldk->slck", recv_rows, up_piece, preferred_element_type=jnp.float32)
    up_term = up_term + jnp.einsum(
        "slcj,lsjk->slck",
        recv_low[..., ADAPTER_RANK:],
        table_split[:, :, ADAPTER_RANK:],
        preferred_element_type=jnp.float32,
    )
    hidden = (jax.nn.silu(gate_term) * up_term).astype(jnp.bfloat16)
    down_whole = lax.all_gather(down_weight, "tensor", axis=2, tiled=True)
    unit_output = jnp.einsum(
        "slck,ldk->slcd", hidden, down_whole, preferred_element_type=jnp.float32
    ).astype(jnp.bfloat16)
    weights_flat = router_weight.reshape(entries)
    returned = lax.all_to_all(unit_output, "dp", split_axis=0, concat_axis=0, tiled=True)
    unit_table = returned.reshape(2 * experts_all * quarter, width)
    lower_slot = jnp.where(entry_mine, slot_part, 0)
    route_gain = jnp.where(entry_mine, weights_flat, 0.0)
    combined = combine_routes(
        unit_table, lower_slot, experts_all * quarter, route_gain, tok_rows, topk
    )
    summed = lax.psum_scatter(combined, "tensor", scatter_dimension=1, tiled=True)
    return summed.astype(jnp.bfloat16)


def solution(mesh):
    in_specs = (
        P("dp", None),
        P(),
        P(),
        P("dp", None),
        P("dp", None),
        P("dp", None, "tensor"),
        P("dp", None, "tensor"),
        P("dp", None, "tensor"),
        P("tensor", "dp"),
        P("dp", None, "tensor"),
    )
    out_specs = P("dp", "tensor")
    return jax.shard_map(
        per_device, mesh=mesh, in_specs=in_specs, out_specs=out_specs, check_vma=False
    )
```

profile of v0, /device:TPU:0, one launch (start us, length us, event | category | flops | bytes accessed | tf_op | source)
XLA Modules:
  0.0 988.3 jit_solution(2396284120542666581)
XLA Ops:
  6.5 1.6 copy.136
  8.2 0.7 all-gather.9.cloned.1.call-update
  8.9 0.7 broadcast_multiply_fusion.1
  9.9 42.5 %all-gather.11.cloned.1.call-done = bf16[2048,2,128]{2,0,1:T(8,128)(2,1)} async-done(((bf16[256,2,128]{2,0,1:T(8,128)(2,1)}), bf16[2048,2,128]{2,0,1:T(8,128)(2,1)}) %all-gather.11.cloned.1.call-update) | async-done | bytes 1048592 | tf_op jit(solution)/shard_map/all_gather | solution.py:81
  52.5 5.7 gather_fusion.3
  58.2 7.6 broadcast_select_fusion
  65.8 10.3 %copy.137 = bf16[16,2048,128]{2,0,1:T(8,128)(2,1)} copy(bf16[16,2048,128]{2,1,0:T(8,128)(2,1)} %broadcast_select_fusion) | data formatting | bytes 16777216 | tf_op jit(solution)/shard_map/jit(_take)/select_n | solution.py:83
  76.1 4.2 gather_fusion.4
  80.4 1.7 select_bitcast_fusion
  82.7 0.5 all-gather.15.cloned.1.call-update
  84.3 0.6 dynamic_slice.11
  84.9 0.6 dynamic_slice.9
  85.4 0.6 iota_compare_fusion.3
  86.1 6.5 gather_fusion
  92.8 18.0 %reduce-window.6 = s32[64,8,128]{2,1,0:T(8,128)S(1)} reduce-window(s32[64,8,128]{2,1,0:T(8,128)S(1)} %fusion.29, s32[]{:T(128)} %constant.103.clone.1), window={size=1x1x128 pad=0_0x0_0x127_0}, to_apply=%region_0.0 | reduce-window | flops 8323072 | bytes 524292 | tf_op jit(solution)/shard_map/reduce-window
  112.8 4.3 scatter_custom_fusion
  117.1 2.5 gather_fusion.1
  119.6 2.4 fusion.16
  122.0 11.2 %psum.7 = bf16[128,32]{0,1:T(8,128)(2,1)S(1)} all-reduce(f32[128,32]{0,1:T(8,128)S(1)} %fusion.16), channel_id=1, replica_groups=mesh['dp'=8,'tensor'=4] {'tensor'}, use_global_device_ids=true, to_apply=%region_4.5 | all-reduce | flops 4096 | bytes 24576 | tf_op jit(solution)/shard_map/psum | solution.py:52
  133.3 1.5 gather_fusion.2
  135.0 0.8 reshape.478
  135.9 3.9 all-to-all-start.1
  139.7 2.2 pad_maximum_fusion
  142.0 6.1 reshape.409
  148.1 8.0 copy.130
  156.1 6.0 all-to-all-start
  162.5 3.4 fusion.44
  165.9 2.6 fusion.10
  168.5 2.6 fusion.12
  171.1 72.0 %all-to-all-done = bf16[8,16,7,2048]{3,1,2,0:T(8,128)(2,1)} async-done(((bf16[8,16,7,2048]{3,1,2,0:T(8,128)(2,1)}), bf16[8,16,7,2048]{3,1,2,0:T(8,128)(2,1)}, u32[]{:S(2)}, u32[]{:S(2)}) %all-to-all-start) | async-done | bytes 3670048 | tf_op jit(solution)/shard_map/all_to_all | solution.py:78
  243.1 103.9 %all-gather.7.cloned.1.call-done = bf16[16,2048,512]{2,1,0:T(8,128)(2,1)} async-done(((bf16[16,2048,128]{2,1,0:T(8,128)(2,1)}), bf16[16,2048,512]{2,1,0:T(8,128)(2,1)}) %all-gather.7.cloned.1.call-update) | async-done | bytes 33554448 | tf_op jit(solution)/shard_map/all_gather | solution.py:88
  347.0 19.5 %fusion.4 = f32[16,8,7,512]{3,1,2,0:T(8,128)S(1)} fusion(bf16[16,2048,512]{2,1,0:T(8,128)(2,1)} %all-gather.7.cloned.1.call-done, bf16[8,16,7,2048]{3,1,2,0:T(8,128)(2,1)} %all-to-all-done), kind=kOutput, calls=%fused_computation.11 | convolution fusion | flops 1879048192 | bytes 39059456 | tf_op jit(solution)/shard_map/slcd,ldk->slck/dot_general | solution.py:92
  366.5 188.0 %all-gather.15.cloned.1.call-done = bf16[16,2048,512]{2,1,0:T(8,128)(2,1)} async-done(((bf16[16,2048,128]{2,1,0:T(8,128)(2,1)}), bf16[16,2048,512]{2,1,0:T(8,128)(2,1)}) %all-gather.15.cloned.1.call-update) | async-done | bytes 33554448 | tf_op jit(solution)/shard_map/all_gather | solution.py:89
  554.5 23.0 %fusion.2 = f32[16,8,7,512]{3,1,2,0:T(8,128)} fusion(bf16[16,2048,512]{2,1,0:T(8,128)(2,1)} %all-gather.15.cloned.1.call-done, bf16[8,16,7,2048]{3,1,2,0:T(8,128)(2,1)} %all-to-all-done), kind=kOutput, calls=%fused_computation.9 | convolution fusion | flops 1879048192 | bytes 39059456 | tf_op jit(solution)/shard_map/slcd,ldk->slck/dot_general | solution.py:101
  577.5 7.7 fusion.15
  585.2 176.8 %all-gather.17.cloned.1.call-done = bf16[16,2048,512]{2,1,0:T(8,128)(2,1)} async-done(((bf16[16,2048,128]{2,1,0:T(8,128)(2,1)}), bf16[16,2048,512]{2,1,0:T(8,128)(2,1)}) %all-gather.17.cloned.1.call-update) | async-done | bytes 33554448 | tf_op jit(solution)/shard_map/all_gather | solution.py:109
  762.0 17.2 %convert_bitcast_fusion = bf16[8,16,7,2048]{3,0,2,1:T(8,128)(2,1)} fusion(bf16[16,2048,512]{2,1,0:T(8,128)(2,1)} %all-gather.17.cloned.1.call-done, bf16[8,16,7,512]{3,1,2,0:T(8,128)(2,1)S(1)} %fusion.15), kind=kOutput, calls=%fused_computation.16 | convolution fusion | flops 1880883200 | bytes 38141952 | tf_op jit(solution)/shard_map/slck,ldk->slcd/dot_general | solution.py:110
  779.2 5.9 copy.147
  785.0 5.5 all-to-all-start.2
  791.3 81.7 %all-to-all-done.2 = bf16[8,16,7,2048]{3,1,2,0:T(8,128)(2,1)} async-done(((bf16[8,16,7,2048]{3,1,2,0:T(8,128)(2,1)}), bf16[8,16,7,2048]{3,1,2,0:T(8,128)(2,1)}, u32[]{:S(2)}, u32[]{:S(2)}) %all-to-all-start.2) | async-done | bytes 3670048 | tf_op jit(solution)/shard_map/all_to_all | solution.py:114
  873.0 6.4 copy.148
  879.4 6.3 reshape.412
  885.7 18.9 %gather_fusion.5 = bf16[2048,2048]{1,0:T(8,128)(2,1)} fusion(bf16[896,2048]{1,0:T(8,128)(2,1)} %reshape.412, s32[2048]{0:T(1024)S(1)} %broadcast_clamp_fusion), kind=kCustom, calls=%fused_computation.5 | custom fusion | bytes 16785408 | tf_op jit(solution)/shard_map/gather | solution.py:14
  904.6 18.1 %reshape.472 = f32[128,8,2,2048]{3,2,1,0:T(2,128)} reshape(bf16[2048,2048]{1,0:T(8,128)(2,1)} %gather_fusion.5) | data formatting | bytes 25165824 | tf_op jit(solution)/shard_map/convert_element_type | solution.py:14
  922.7 26.2 %reduce_sum.28 = f32[128,8,2048]{2,1,0:T(8,128)} reduce(f32[128,8,2,2048]{3,2,1,0:T(2,128)} %reshape.472, f32[]{:T(128)} %constant.125.clone.1), dimensions={2}, to_apply=%region_5.6 | reduce | flops 2097152 | bytes 25165828 | tf_op jit(solution)/shard_map/reduce_sum | solution.py:15
  948.9 7.4 multiply_reduce_fusion
  956.4 23.2 %reduce-scatter.2.cloned.1.call-done = f32[128,512]{1,0:T(8,128)} async-done(((f32[128,2048]{1,0:T(8,128)}), f32[128,512]{1,0:T(8,128)}) %reduce-scatter.2.cloned.1.call-update) | async-done | bytes 262160 | tf_op jit(solution)/shard_map/reduce_scatter | solution.py:121
  979.5 1.6 convert_element_type.35
  (76 shorter events, 4.7 us)
Async XLA Ops:
  6.5 45.9 %all-gather.11.cloned.1.call-start = ((), (), s32[]{:S(2)}) async-start(), calls=%async_computation.6 | async-start | bytes 1179648 | tf_op jit(solution)/shard_map/all_gather | solution.py:81
  8.1 111.5 %all-gather.9.cloned.1.call-start = ((), (), s32[]{:S(2)}) async-start(), calls=%async_computation.5 | async-start | bytes 2359296 | tf_op jit(solution)/shard_map/all_gather | solution.py:45
  8.9 153.6 %all-gather.13.cloned.1.call-start = ((), (), s32[]{:S(2)}) async-start(), calls=%async_computation.7 | async-start | bytes 5242880 | tf_op jit(solution)/shard_map/all_gather | solution.py:90
  82.1 264.9 %all-gather.7.cloned.1.call-start = ((), (), s32[]{:S(2)}) async-start(), calls=%async_computation.4 | async-start | bytes 41943040 | tf_op jit(solution)/shard_map/all_gather | solution.py:88
  82.7 471.8 %all-gather.15.cloned.1.call-start = ((), (), s32[]{:S(2)}) async-start(), calls=%async_computation.8 | async-start | bytes 41943040 | tf_op jit(solution)/shard_map/all_gather | solution.py:89
  83.3 0.7 copy-start.1
  83.3 1.0 copy-start.3
  83.3 1.6 copy-start.4
  83.3 678.7 %all-gather.17.cloned.1.call-start = ((), (), s32[]{:S(2)}) async-start(), calls=%async_computation.9 | async-start | bytes 41943040 | tf_op jit(solution)/shard_map/all_gather | solution.py:109
  84.0 27.8 %copy-start.2 = (f32[128,8]{0,1:T(8,128)S(1)}, f32[128,8]{0,1:T(8,128)}, u32[]{:S(2)}) copy-start(f32[128,8]{0,1:T(8,128)} %param.14) | copy-start | bytes 12292
  84.0 28.7 %copy-start = (bf16[128,2048]{1,0:T(8,128)(2,1)S(1)}, bf16[128,2048]{1,0:T(8,128)(2,1)}, u32[]{:S(2)}) copy-start(bf16[128,2048]{1,0:T(8,128)(2,1)} %param.10) | copy-start | bytes 1572868
  135.9 20.3 %all-to-all-start.1 = ((bf16[8,2,1792]{2,1,0:T(2,128)(2,1)}), bf16[8,2,1792]{2,1,0:T(2,128)(2,1)S(1)}, u32[]{:S(2)}, u32[]{:S(2)}) async-start(bf16[8,2,1792]{2,1,0:T(2,128)(2,1)} %reshape.478), calls=%async_computation.1 | async-start | bytes 114688 | tf_op jit(solution)/shard_map/all_to_all | solution.py:79
  156.1 87.0 %all-to-all-start = ((bf16[8,16,7,2048]{3,1,2,0:T(8,128)(2,1)}), bf16[8,16,7,2048]{3,1,2,0:T(8,128)(2,1)}, u32[]{:S(2)}, u32[]{:S(2)}) async-start(bf16[8,16,7,2048]{3,1,2,0:T(8,128)(2,1)} %copy.130), calls=%async_computation | async-start | bytes 7340032 | tf_op jit(solution)/shard_map/all_to_all | solution.py:78
  785.0 88.0 %all-to-all-start.2 = ((bf16[8,16,7,2048]{3,1,2,0:T(8,128)(2,1)}), bf16[8,16,7,2048]{3,1,2,0:T(8,128)(2,1)}, u32[]{:S(2)}, u32[]{:S(2)}) async-start(bf16[8,16,7,2048]{3,1,2,0:T(8,128)(2,1)} %copy.147), calls=%async_computation.2 | async-start | bytes 7340032 | tf_op jit(solution)/shard_map/all_to_all | solution.py:114
  790.5 189.0 %reduce-scatter.2.cloned.1.call-start = ((), (), s32[]{:S(2)}) async-start(), calls=%async_computation.10 | async-start | bytes 1310720 | tf_op jit(solution)/shard_map/reduce_scatter | solution.py:121
Sparse Core Ops, SparseCore 0:
  9.5 42.8 all-gather.10
  54.5 49.8 all-gather.8
  106.0 33.4 all-gather.12
  140.9 206.0 all-gather.6
  348.4 206.0 all-gather.14
  555.9 206.0 all-gather.16
  956.5 23.0 reduce-scatter.1
where the time goes:
time: 997 us; the launch traced here: 988 us
  waiting for transfers between devices  691 us (69%)
  local copies, waits for them, and re-layouts  114 us (11%)
  other arithmetic  74.5 us (7%)
  matrix products  67.3 us (7%)
  starting transfers between devices  15.6 us (2%)
  between operations  14.8 us (1%)
  blocking collectives  11.2 us (1%)
    all_gather x1, waiting for transfers between devices, per_device(): up_piece = lax.all_gather(up_weight, 'tensor', axis=2, tiled=True)  188 us
    all_gather x1, waiting for transfers between devices, per_device(): down_whole = lax.all_gather(down_weight, 'tensor', axis=2, tiled=True)  177 us
    all_gather x1, waiting for transfers between devices, per_device(): gate_piece = lax.all_gather(gate_weight, 'tensor', axis=2, tiled=True)  104 us
    all_to_all x1, waiting for transfers between devices, per_device(): lax.all_to_all(unit_output, 'dp', split_axis=0, concat_axis=0, tiled=True)  81.7 us
    all_to_all x1, waiting for transfers between devices, per_device(): lax.all_to_all(send_rows, 'dp', split_axis=0, concat_axis=0, tiled=True)  72 us
    all_gather x1, waiting for transfers between devices, per_device(): every_table = lax.all_gather(adapter_output_maps, 'dp', axis=0, tiled=True)  42.5 us
    reduce_sum x1, other arithmetic, combine_routes(): summed_pair = jnp.sum(pair_rows, axis=2)  26.2 us
    reduce_scatter x1, waiting for transfers between devices, per_device(): lax.psum_scatter(combined, 'tensor', scatter_dimension=1, tiled=True)  23.2 us
  transfers between devices with their start and end apart: 10, of which 7 were waited for; matrix products, arithmetic and copies ran while one was open for 15% of the time, Pallas kernels for 0%

commit v1 on v0

--- a/solution.py
+++ b/solution.py
@@ -5,6 +5,42 @@
 
 ADAPTER_RANK = 16
 CAP = 28
+
+
+def convert_the_vectors(vector, which_dim, xin, row_dim):
+    a_now = jax.lax.axis_size("tensor")
+    x_next = jax.lax.axis_index("tensor")
+    piece_out, piece_next, back = (a_now, x_next, vector.shape[which_dim])
+    samples = [(no, (no + 1) % piece_out) for no in range(piece_out)]
+    sides = [(w, h) for h, w in samples]
+    part_now = jax.lax.ppermute(vector, "tensor", samples)
+    wide_out = jax.lax.ppermute(vector, "tensor", sides)
+    part_next, e_next = (part_now, wide_out)
+    val2 = xin(vector, piece_next * back)
+    g_now = val2.shape[row_dim]
+    row_out = jnp.zeros(
+        (*val2.shape[:row_dim], piece_out * g_now, *val2.shape[row_dim + 1 :]), val2.dtype
+    )
+
+    def lanes_lay(row_out, val2, z_new):
+        arr_next = lax.dynamic_update_slice_in_dim(row_out, val2, z_new * g_now, axis=row_dim)
+        return arr_next
+
+    row_out = lanes_lay(row_out, val2, piece_next)
+    for src_i in range(1, piece_out // 2 + 1):
+        carry, y_new = ((piece_next - src_i) % piece_out, (piece_next + src_i) % piece_out)
+        item_now = (part_next, e_next)
+        if src_i < piece_out // 2:
+            part_next, e_next = (
+                jax.lax.ppermute(part_next, "tensor", samples),
+                jax.lax.ppermute(e_next, "tensor", sides),
+            )
+        later = xin(item_now[0], carry * back)
+        row_out = lanes_lay(row_out, later, carry)
+        if 2 * src_i < piece_out:
+            arr_out = xin(item_now[1], y_new * back)
+            row_out = lanes_lay(row_out, arr_out, y_new)
+    return row_out
 
 
 def combine_routes(unit_table, lower_slot, shift_half, route_gain, tok_rows, topk):
@@ -85,12 +121,16 @@
         request_adapter[:, None] * double_rank + jnp.arange(double_rank)[None, :]
     ).reshape(dp_count * double_rank)
     source_tables = jnp.take(half_tables, source_rows, axis=1)
-    gate_piece = lax.all_gather(gate_weight, "tensor", axis=2, tiled=True)
     up_piece = lax.all_gather(up_weight, "tensor", axis=2, tiled=True)
     table_piece = lax.all_gather(source_tables, "tensor", axis=2, tiled=True)
     table_split = table_piece.reshape(units_local, dp_count, double_rank, table_piece.shape[2])
-    gate_term = jnp.einsum(
-        "slcd,ldk->slck", recv_rows, gate_piece, preferred_element_type=jnp.float32
+    gate_term = convert_the_vectors(
+        gate_weight,
+        2,
+        lambda shard, at: jnp.einsum(
+            "slcd,ldk->slck", recv_rows, shard, preferred_element_type=jnp.float32
+        ),
+        3,
     )
     gate_term = gate_term + jnp.einsum(
         "slcj,lsjk->slck",

time: 997 us -> 981 us (0.984)
  waiting for transfers between devices: 691 us -> 529 us
  blocking collectives: 11.2 us -> 140 us
  matrix products: 67.3 us -> 90.6 us
    ppermute x0 -> x3, waiting for transfers between devices: none -> 229 us  [the longest x1 229 us: convert_the_vectors(): wide_out = jax.lax.ppermute(vector, 'tensor', sides)]
    all_gather x1, waiting for transfers between devices: 188 us -> 0.02 us  [per_device(): up_piece = lax.all_gather(up_weight, 'tensor', axis=2, tiled=True)]
    psum x1, blocking collectives: 11.2 us -> 140 us  [per_device(): low_rank = lax.psum(partial_z, 'tensor').astype(jnp.bfloat16)]
    all_gather x1, waiting for transfers between devices: 177 us -> 69.4 us  [per_device(): down_whole = lax.all_gather(down_weight, 'tensor', axis=2, tiled=True)]
    all_gather x1 -> x0, waiting for transfers between devices: 104 us -> none  [per_device(): gate_piece = lax.all_gather(gate_weight, 'tensor', axis=2, tiled=True)]
    dot_general x1 -> x4, matrix products: 19.5 us -> 43.8 us  [per_device(): jnp.einsum('slcd,ldk->slck', recv_rows, shard, preferred_element_type=jnp...]
  transfers between devices with their start and end apart: 10 -> 12, of which waited for: 7 -> 6; matrix products, arithmetic and copies ran while one was open for 15% -> 17% of each run, Pallas kernels for 0% -> 0%
where the time goes in v1:
time: 981 us; the launch traced here: 972 us
  waiting for transfers between devices  529 us (54%)
  blocking collectives  140 us (14%)
  local copies, waits for them, and re-layouts  115 us (12%)
  matrix products  90.6 us (9%)
  other arithmetic  66.8 us (7%)
  starting transfers between devices  15.1 us (2%)
  between operations  15.1 us (2%)
    ppermute x1, waiting for transfers between devices, convert_the_vectors(): wide_out = jax.lax.ppermute(vector, 'tensor', sides)  229 us
    psum x1, blocking collectives, per_device(): low_rank = lax.psum(partial_z, 'tensor').astype(jnp.bfloat16)  140 us
    all_to_all x1, waiting for transfers between devices, per_device(): lax.all_to_all(unit_output, 'dp', split_axis=0, concat_axis=0, tiled=True)  81.7 us
    all_to_all x1, waiting for transfers between devices, per_device(): lax.all_to_all(send_rows, 'dp', split_axis=0, concat_axis=0, tiled=True)  81 us
    all_gather x1, waiting for transfers between devices, per_device(): down_whole = lax.all_gather(down_weight, 'tensor', axis=2, tiled=True)  69.4 us
    dot_general x4, matrix products, per_device(): jnp.einsum('slcd,ldk->slck', recv_rows, shard, preferred_element_type=jnp...  43.8 us
    all_gather x1, waiting for transfers between devices, per_device(): every_table = lax.all_gather(adapter_output_maps, 'dp', axis=0, tiled=True)  42.5 us
    reduce_sum x1, other arithmetic, combine_routes(): summed_pair = jnp.sum(pair_rows, axis=2)  26.2 us
  transfers between devices with their start and end apart: 12, of which 6 were waited for; matrix products, arithmetic and copies ran while one was open for 17% of the time, Pallas kernels for 0%

profile of v1, /device:TPU:0, one launch (start us, length us, event | category | flops | bytes accessed | tf_op | source)
XLA Modules:
  0.0 971.9 jit_solution(5759900859813038929)
XLA Ops:
  6.5 1.6 copy.138
  8.2 0.7 all-gather.6.cloned.1.call-update
  8.9 0.7 broadcast_multiply_fusion.1
  9.9 42.5 %all-gather.8.cloned.1.call-done = bf16[2048,2,128]{2,0,1:T(8,128)(2,1)} async-done(((bf16[256,2,128]{2,0,1:T(8,128)(2,1)}), bf16[2048,2,128]{2,0,1:T(8,128)(2,1)}) %all-gather.8.cloned.1.call-update) | async-done | bytes 1048592 | tf_op jit(solution)/shard_map/all_gather | solution.py:117
  52.5 5.7 gather_fusion.3
  58.2 7.6 broadcast_select_fusion
  65.8 10.3 %copy.139 = bf16[16,2048,128]{2,0,1:T(8,128)(2,1)} copy(bf16[16,2048,128]{2,1,0:T(8,128)(2,1)} %broadcast_select_fusion) | data formatting | bytes 16777216 | tf_op jit(solution)/shard_map/jit(_take)/select_n | solution.py:119
  76.1 4.2 gather_fusion.4
  80.4 1.7 select_bitcast_fusion
  84.3 0.6 dynamic_slice.9
  84.9 0.6 iota_compare_fusion.3
  85.5 6.5 gather_fusion
  92.2 18.0 %reduce-window.6 = s32[64,8,128]{2,1,0:T(8,128)S(1)} reduce-window(s32[64,8,128]{2,1,0:T(8,128)S(1)} %fusion.60, s32[]{:T(128)} %constant.128.clone.1), window={size=1x1x128 pad=0_0x0_0x127_0}, to_apply=%region_0.0 | reduce-window | flops 8323072 | bytes 524292 | tf_op jit(solution)/shard_map/reduce-window
  111.5 4.3 scatter_custom_fusion
  115.9 2.5 gather_fusion.1
  119.0 2.4 fusion.47
  121.5 140.2 %psum.7 = bf16[128,32]{0,1:T(8,128)(2,1)S(1)} all-reduce(f32[128,32]{0,1:T(8,128)S(1)} %fusion.47), channel_id=1, replica_groups=mesh['dp'=8,'tensor'=4] {'tensor'}, use_global_device_ids=true, to_apply=%region_4.5 | all-reduce | flops 4096 | bytes 24576 | tf_op jit(solution)/shard_map/psum | solution.py:88
  261.8 1.5 gather_fusion.2
  263.5 0.8 reshape.481
  264.3 3.6 all-to-all-start.1
  267.9 2.3 pad_maximum_fusion
  270.2 6.0 reshape.409
  276.2 6.6 copy.126
  282.7 6.0 all-to-all-start
  289.4 0.8 fusion.76
  290.1 81.0 %all-to-all-done = bf16[8,16,7,2048]{3,1,2,0:T(8,128)(2,1)} async-done(((bf16[8,16,7,2048]{3,1,2,0:T(8,128)(2,1)}), bf16[8,16,7,2048]{3,1,2,0:T(8,128)(2,1)}, u32[]{:S(2)}, u32[]{:S(2)}) %all-to-all-start) | async-done | bytes 3670048 | tf_op jit(solution)/shard_map/all_to_all | solution.py:114
  371.1 8.8 fusion.27
  380.4 4.0 fusion.75
  384.4 2.6 fusion.19
  387.0 8.8 fusion.32
  395.9 229.0 %collective-permute-done.1 = bf16[16,2048,128]{2,1,0:T(8,128)(2,1)} collective-permute-done((bf16[16,2048,128]{2,1,0:T(8,128)(2,1)}, bf16[16,2048,128]{2,1,0:T(8,128)(2,1)}, u32[]{:S(2)}, u32[]{:S(2)}) %collective-permute-start.1) | collective-permute-done | bytes 8388640 | tf_op jit(solution)/shard_map/ppermute | solution.py:17
  625.0 17.5 %fusion.37 = f32[8,16,7,128]{3,0,2,1:T(8,128)S(1)} fusion(bf16[16,2048,128]{2,1,0:T(8,128)(2,1)} %collective-permute-done.1, bf16[8,16,7,2048]{3,1,2,0:T(8,128)(2,1)} %all-to-all-done), kind=kOutput, calls=%fused_computation.37 | convolution fusion | flops 469762048 | bytes 12517376 | tf_op jit(solution)/shard_map/slcd,ldk->slck/dot_general | solution.py:130
  642.7 8.8 fusion.42
  651.7 20.1 %fusion.2 = f32[16,8,7,512]{3,2,0,1:T(8,128)} fusion(bf16[16,2048,512]{2,1,0:T(8,128)(2,1)} %all-gather.12.cloned.1.call-done, bf16[8,16,7,2048]{3,1,2,0:T(8,128)(2,1)} %all-to-all-done), kind=kOutput, calls=%fused_computation.9 | convolution fusion | flops 1879048192 | bytes 39059456 | tf_op jit(solution)/shard_map/slcd,ldk->slck/dot_general | solution.py:141
  671.8 4.7 fusion.24
  676.5 69.4 %all-gather.14.cloned.1.call-done = bf16[16,2048,512]{2,1,0:T(8,128)(2,1)} async-done(((bf16[16,2048,128]{2,1,0:T(8,128)(2,1)}), bf16[16,2048,512]{2,1,0:T(8,128)(2,1)}) %all-gather.14.cloned.1.call-update) | async-done | bytes 33554448 | tf_op jit(solution)/shard_map/all_gather | solution.py:149
  745.9 17.0 %convert_bitcast_fusion = bf16[8,16,7,2048]{3,0,2,1:T(8,128)(2,1)} fusion(bf16[16,2048,512]{2,1,0:T(8,128)(2,1)} %all-gather.14.cloned.1.call-done, bf16[8,16,7,512]{3,2,1,0:T(8,128)(2,1)S(1)} %fusion.24), kind=kOutput, calls=%fused_computation.23 | convolution fusion | flops 1880883200 | bytes 38141952 | tf_op jit(solution)/shard_map/slck,ldk->slcd/dot_general | solution.py:150
  762.9 5.9 copy.146
  768.7 4.5 all-to-all-start.2
  774.3 81.7 %all-to-all-done.2 = bf16[8,16,7,2048]{3,1,2,0:T(8,128)(2,1)} async-done(((bf16[8,16,7,2048]{3,1,2,0:T(8,128)(2,1)}), bf16[8,16,7,2048]{3,1,2,0:T(8,128)(2,1)}, u32[]{:S(2)}, u32[]{:S(2)}) %all-to-all-start.2) | async-done | bytes 3670048 | tf_op jit(solution)/shard_map/all_to_all | solution.py:154
  855.9 6.4 copy.147
  862.3 6.1 reshape.412
  868.4 18.9 %gather_fusion.5 = bf16[2048,2048]{1,0:T(8,128)(2,1)} fusion(bf16[896,2048]{1,0:T(8,128)(2,1)} %reshape.412, s32[2048]{0:T(1024)S(1)} %broadcast_clamp_fusion), kind=kCustom, calls=%fused_computation.5 | custom fusion | bytes 16785408 | tf_op jit(solution)/shard_map/gather | solution.py:50
  887.3 18.1 %reshape.472 = f32[128,8,2,2048]{3,2,1,0:T(2,128)} reshape(bf16[2048,2048]{1,0:T(8,128)(2,1)} %gather_fusion.5) | data formatting | bytes 25165824 | tf_op jit(solution)/shard_map/convert_element_type | solution.py:50
  905.4 26.2 %reduce_sum.28 = f32[128,8,2048]{2,1,0:T(8,128)} reduce(f32[128,8,2,2048]{3,2,1,0:T(2,128)} %reshape.472, f32[]{:T(128)} %constant.123.clone.1), dimensions={2}, to_apply=%region_5.6 | reduce | flops 2097152 | bytes 25165828 | tf_op jit(solution)/shard_map/reduce_sum | solution.py:51
  931.6 7.4 multiply_reduce_fusion
  939.0 24.0 %reduce-scatter.2.cloned.1.call-done = f32[128,512]{1,0:T(8,128)} async-done(((f32[128,2048]{1,0:T(8,128)}), f32[128,512]{1,0:T(8,128)}) %reduce-scatter.2.cloned.1.call-update) | async-done | bytes 262160 | tf_op jit(solution)/shard_map/reduce_scatter | solution.py:161
  963.0 1.6 convert_element_type.35
  (86 shorter events, 6.9 us)
Async XLA Ops:
  6.5 45.9 %all-gather.8.cloned.1.call-start = ((), (), s32[]{:S(2)}) async-start(), calls=%async_computation.5 | async-start | bytes 1179648 | tf_op jit(solution)/shard_map/all_gather | solution.py:117
  8.1 110.9 %all-gather.6.cloned.1.call-start = ((), (), s32[]{:S(2)}) async-start(), calls=%async_computation.4 | async-start | bytes 2359296 | tf_op jit(solution)/shard_map/all_gather | solution.py:81
  8.9 371.5 %all-gather.10.cloned.1.call-start = ((), (), s32[]{:S(2)}) async-start(), calls=%async_computation.6 | async-start | bytes 5242880 | tf_op jit(solution)/shard_map/all_gather | solution.py:125
  82.1 569.6 %all-gather.12.cloned.1.call-start = ((), (), s32[]{:S(2)}) async-start(), calls=%async_computation.7 | async-start | bytes 41943040 | tf_op jit(solution)/shard_map/all_gather | solution.py:124
  82.7 0.7 copy-start.1
  82.7 1.0 copy-start.3
  82.7 1.6 copy-start.4
  82.7 663.2 %all-gather.14.cloned.1.call-start = ((), (), s32[]{:S(2)}) async-start(), calls=%async_computation.8 | async-start | bytes 41943040 | tf_op jit(solution)/shard_map/all_gather | solution.py:149
  83.3 27.8 %copy-start.2 = (f32[128,8]{0,1:T(8,128)S(1)}, f32[128,8]{0,1:T(8,128)}, u32[]{:S(2)}) copy-start(f32[128,8]{0,1:T(8,128)} %param.14) | copy-start | bytes 12292
  83.3 28.1 %copy-start = (bf16[128,2048]{1,0:T(8,128)(2,1)S(1)}, bf16[128,2048]{1,0:T(8,128)(2,1)}, u32[]{:S(2)}) copy-start(bf16[128,2048]{1,0:T(8,128)(2,1)} %param.10) | copy-start | bytes 1572868
  83.3 205.4 %collective-permute-start = (bf16[16,2048,128]{2,1,0:T(8,128)(2,1)}, bf16[16,2048,128]{2,1,0:T(8,128)(2,1)}, u32[]{:S(2)}, u32[]{:S(2)}) collective-permute-start(bf16[16,2048,128]{2,1,0:T(8,128)(2,1)} %param.15), channel_id=1, source_target_pairs={{0,1},{1,2},{2,3},{3,0},{4,5},{5,6},{6,7},{7,4},{8,9},{9,10},{10,1... | collective-permute-start | bytes 25165832 | tf_op jit(solution)/shard_map/ppermute | solution.py:16
  264.3 18.4 %all-to-all-start.1 = ((bf16[8,2,1792]{2,1,0:T(2,128)(2,1)}), bf16[8,2,1792]{2,1,0:T(2,128)(2,1)S(1)}, u32[]{:S(2)}, u32[]{:S(2)}) async-start(bf16[8,2,1792]{2,1,0:T(2,128)(2,1)} %reshape.481), calls=%async_computation.1 | async-start | bytes 114688 | tf_op jit(solution)/shard_map/all_to_all | solution.py:115
  282.7 88.4 %all-to-all-start = ((bf16[8,16,7,2048]{3,1,2,0:T(8,128)(2,1)}), bf16[8,16,7,2048]{3,1,2,0:T(8,128)(2,1)}, u32[]{:S(2)}, u32[]{:S(2)}) async-start(bf16[8,16,7,2048]{3,1,2,0:T(8,128)(2,1)} %copy.126), calls=%async_computation | async-start | bytes 7340032 | tf_op jit(solution)/shard_map/all_to_all | solution.py:114
  288.7 336.3 %collective-permute-start.1 = (bf16[16,2048,128]{2,1,0:T(8,128)(2,1)}, bf16[16,2048,128]{2,1,0:T(8,128)(2,1)}, u32[]{:S(2)}, u32[]{:S(2)}) collective-permute-start(bf16[16,2048,128]{2,1,0:T(8,128)(2,1)} %param.15), channel_id=1, source_target_pairs={{1,0},{2,1},{3,2},{0,3},{5,4},{6,5},{7,6},{4,7},{9,8},{10,9},{11,1... | collective-permute-start | bytes 25165832 | tf_op jit(solution)/shard_map/ppermute | solution.py:17
  288.7 353.9 %collective-permute-start.2 = (bf16[16,2048,128]{2,1,0:T(8,128)(2,1)}, bf16[16,2048,128]{2,1,0:T(8,128)(2,1)}, u32[]{:S(2)}, u32[]{:S(2)}) collective-permute-start(bf16[16,2048,128]{2,1,0:T(8,128)(2,1)} %collective-permute-done), channel_id=1, source_target_pairs={{0,1},{1,2},{2,3},{3,0},{4,5},{5,6},{6,7},{7,4},{8,9},{9,10},{10,1... | collective-permute-start | bytes 25165832 | tf_op jit(solution)/shard_map/ppermute | solution.py:35
  768.7 87.2 %all-to-all-start.2 = ((bf16[8,16,7,2048]{3,1,2,0:T(8,128)(2,1)}), bf16[8,16,7,2048]{3,1,2,0:T(8,128)(2,1)}, u32[]{:S(2)}, u32[]{:S(2)}) async-start(bf16[8,16,7,2048]{3,1,2,0:T(8,128)(2,1)} %copy.146), calls=%async_computation.2 | async-start | bytes 7340032 | tf_op jit(solution)/shard_map/all_to_all | solution.py:154
  773.3 189.7 %reduce-scatter.2.cloned.1.call-start = ((), (), s32[]{:S(2)}) async-start(), calls=%async_computation.9 | async-start | bytes 1310720 | tf_op jit(solution)/shard_map/reduce_scatter | solution.py:161
Sparse Core Ops, SparseCore 0:
  9.5 42.8 all-gather.7
  54.5 49.8 all-gather.5
  105.9 44.6 all-gather.9
  152.0 320.2 all-gather.11
  473.7 272.1 all-gather.13
  939.1 23.8 reduce-scatter.1
